TPU v7x, 32 devices: a whole 2x2x4 slice. The times are simulated.
32 devices in a mesh: seq: 8 (over z, core), head: 4 (over y, x).
Axes of the slice: x: 2, y: 2, z: 4, core: 2. Of those that a mesh axis runs over, the one named last changes fastest.
Arguments:
- mixer_input: bfloat16 [2048, 4096], P('seq', 'head'), may hold values from -600 to 600
- gate_input: bfloat16 [2048, 4096], P('seq', 'head'), may hold values from -5 to 5
- b_proj: bfloat16 [2048, 128], P('seq'), may hold values from -0.5 to 0.5
- c_proj: bfloat16 [2048, 128], P('seq'), may hold values from -0.5 to 0.5
- decay_codes: int32 [64, 2048], P('head', 'seq'), may hold values from 1 to 4096
- decay_rates: float32 [64], P('head'), may hold values from 0 to 1
- skip_gain: float32 [64], P('head'), may hold values from 0.5 to 1.5
- norm_gain: float32 [4096], P('head'), may hold values from 0.5 to 1.5
- queries: bfloat16 [2048, 4096], P('seq', 'head'), may hold values from -5 to 5
- keys: bfloat16 [2048, 4096], P('seq', 'head'), may hold values from -5 to 5
Outputs:
- mamba_out: bfloat16 [2048, 4096], P('seq', 'head')
- attn_out: bfloat16 [2048, 4096], P('seq', 'head')
All inputs are finite; a program needn't handle non-finite values.
Results may differ from a plain program's by a relative error of at most 0.013.
Values may be sent and summed in bfloat16 or wider, within the bound.
No kernel may reach another device: no remote copies, remote signals or barrier semaphores. Data moves between devices by JAX's collectives and lax.ppermute only.
A program may use at most 64 MiB of HBM per device.

v0:
```python
import functools
import math
import jax
import jax.numpy as jnp
from jax import lax
from jax.sharding import PartitionSpec as P

HD = 128
CHANNELS_PER_HD = 64
BLOCK = 256
HIGH = lax.Precision.HIGHEST
NEG = -1e30


def carried_in(array, axis, combine, identity):
    devices, mine = (lax.axis_size(axis), lax.axis_index(axis))
    everything = jax.tree.map(
        lambda part, kind: lax.all_gather(part.astype(kind), axis),
        array,
        (jnp.bfloat16, jnp.bfloat16),
    )
    start = jax.tree.map(
        lambda part, zero: jnp.broadcast_to(jnp.asarray(zero, part.dtype), part.shape),
        array,
        identity,
    )

    def hop(k, before):
        reached = k < mine
        new = combine(
            before, jax.tree.map(lambda part, own: part[k].astype(own.dtype), everything, array)
        )
        return jax.tree.map(lambda a, b: jnp.where(reached, a, b), new, before)

    return lax.fori_loop(0, devices, hop, start)


def block_step(state_carry, inputs):
    x_block, b_block, c_block, decay_block = inputs
    running = jnp.cumsum(decay_block, axis=1)
    span = decay_block.shape[1]
    causal = (
        jnp.arange(span, dtype=jnp.int32)[:, None] >= jnp.arange(span, dtype=jnp.int32)[None, :]
    )
    log_gaps = jnp.where(causal[None, :, :], running[:, :, None] - running[:, None, :], NEG)
    decays = jnp.exp(log_gaps)
    match_strength = jnp.dot(c_block, b_block.T, preferred_element_type=jnp.float32)
    x_float = x_block.astype(jnp.float32)
    within = jnp.einsum(
        "hts,shp->thp", decays * match_strength[None, :, :], x_float, precision=HIGH
    )
    c_float = c_block.astype(jnp.float32)
    carried = jnp.exp(running).T[:, :, None] * jnp.einsum(
        "tn,hnp->thp", c_float, state_carry, precision=HIGH
    )
    to_end = jnp.exp(running[:, -1:] - running)
    updated_state = jnp.exp(running[:, -1])[:, None, None] * state_carry + jnp.einsum(
        "hs,sn,shp->hnp", to_end, b_block.astype(jnp.float32), x_float, precision=HIGH
    )
    return (updated_state, within + carried)


def local_scan(x_local, b_local, c_local, log_decay):
    tok_rows = x_local.shape[0]
    heads_local = log_decay.shape[0]
    block_count = tok_rows // BLOCK
    x_blocks = x_local.reshape(block_count, BLOCK, heads_local, CHANNELS_PER_HD)
    b_blocks = b_local.reshape(block_count, BLOCK, b_local.shape[1])
    c_blocks = c_local.reshape(block_count, BLOCK, c_local.shape[1])
    decay_blocks = log_decay.reshape(heads_local, block_count, BLOCK).transpose(1, 0, 2)
    initial = jnp.zeros((heads_local, b_local.shape[1], CHANNELS_PER_HD), jnp.float32)
    final_state, y_blocks = lax.scan(
        block_step, initial, (x_blocks, b_blocks, c_blocks, decay_blocks)
    )
    return (final_state, y_blocks.reshape(tok_rows, heads_local, CHANNELS_PER_HD))


def masked_scores(q_rows, q_pos, k_rows, k_pos):
    score_scale = 1.0 / math.sqrt(k_rows.shape[-1])
    scores = (
        jnp.einsum("qhd,khd->hqk", q_rows, k_rows, preferred_element_type=jnp.float32) * score_scale
    )
    visible = k_pos[None, None, :] <= q_pos[None, :, None]
    return (jnp.where(visible, scores, NEG), visible)


def online_update(group_state, q_rows, q_pos, k_rows, v_rows, k_pos):
    row_top, row_total, weighted_sum = group_state
    scores, visible = masked_scores(q_rows, q_pos, k_rows, k_pos)
    new_top = jnp.maximum(row_top, jnp.max(scores, axis=2))
    rescale = jnp.exp(row_top - new_top)
    weights = jnp.where(visible, jnp.exp(scores - new_top[:, :, None]), 0.0)
    row_total = row_total * rescale + jnp.sum(weights, axis=2)
    weighted_sum = weighted_sum * rescale[:, :, None] + jnp.einsum(
        "hqk,khd->hqd", weights.astype(jnp.bfloat16), v_rows, preferred_element_type=jnp.float32
    )
    return (new_top, row_total, weighted_sum)


def when_visible(state_update, group_state, q_pos, key_offset):
    return lax.cond(key_offset > q_pos[-1], lambda held: held, state_update, group_state)


def on_device(
    mixer_input,
    gate_input,
    b_proj,
    c_proj,
    decay_codes,
    decay_rates,
    skip_gain,
    norm_gain,
    queries,
    keys,
):
    tok_rows = mixer_input.shape[0]
    heads_local = decay_rates.shape[0]
    heads_att = queries.shape[1] // HD
    seq_rank = lax.axis_index("seq")
    own_positions = seq_rank * tok_rows + jnp.arange(tok_rows, dtype=jnp.int32)
    groups = [(queries, own_positions)]
    groups = [(q_rows.reshape(q_rows.shape[0], heads_att, HD), q_pos) for q_rows, q_pos in groups]
    log_decay = -decay_rates[:, None] * decay_codes.astype(jnp.float32)
    local_state, y_local = local_scan(mixer_input, b_proj, c_proj, log_decay)
    total_log = jnp.sum(log_decay, axis=1)

    def combine(earlier, later):
        return (earlier[0] + later[0], jnp.exp(later[0])[:, None, None] * earlier[1] + later[1])

    identity = (jnp.zeros_like(total_log), jnp.zeros_like(local_state))
    _, incoming = carried_in((total_log, local_state), "seq", combine, identity)
    running = jnp.cumsum(log_decay, axis=1)
    carried = jnp.einsum("tn,hnp->thp", c_proj.astype(jnp.float32), incoming, precision=HIGH)
    carried = carried * jnp.exp(running).T[:, :, None]
    x_float = mixer_input.reshape(tok_rows, heads_local, CHANNELS_PER_HD).astype(jnp.float32)
    ssm_out = (y_local + carried + skip_gain[None, :, None] * x_float).reshape(
        tok_rows, heads_local * CHANNELS_PER_HD
    )
    gated = ssm_out * jax.nn.silu(gate_input.astype(jnp.float32))
    squares = lax.psum(jnp.sum(gated * gated, axis=1), "head")
    channels = gated.shape[1] * lax.axis_size("head")
    mamba_out = (
        gated * lax.rsqrt(squares / channels + 1e-05)[:, None] * norm_gain[None, :]
    ).astype(jnp.bfloat16)
    initial = tuple(
        (
            (
                jnp.full((heads_att, q_pos.shape[0]), NEG, jnp.float32),
                jnp.zeros((heads_att, q_pos.shape[0]), jnp.float32),
                jnp.zeros((heads_att, q_pos.shape[0], HD), jnp.float32),
            )
            for _, q_pos in groups
        )
    )
    states = initial
    k_piece = lax.all_gather(keys, "seq", axis=0, tiled=True)
    v_piece = lax.all_gather(mamba_out, "seq", axis=0, tiled=True)
    row_count = k_piece.shape[0]
    block_rows = math.gcd(row_count, 512)

    def one_block(block_id, states):
        key_offset = block_id * block_rows
        k_rows = lax.dynamic_slice_in_dim(k_piece, block_id * block_rows, block_rows, 0).reshape(
            block_rows, heads_att, HD
        )
        v_rows = lax.dynamic_slice_in_dim(v_piece, block_id * block_rows, block_rows, 0).reshape(
            block_rows, heads_att, HD
        )
        k_pos = key_offset + jnp.arange(block_rows, dtype=jnp.int32)
        return tuple(
            (
                when_visible(
                    functools.partial(
                        online_update,
                        q_rows=group[0],
                        q_pos=group[1],
                        k_rows=k_rows,
                        v_rows=v_rows,
                        k_pos=k_pos,
                    ),
                    group_state,
                    group[1],
                    key_offset,
                )
                for group, group_state in zip(groups, states)
            )
        )

    finals = lax.fori_loop(0, row_count // block_rows, one_block, states)
    results = [(group_state[2], group_state[1]) for group_state in finals]
    rows_out = [
        (weighted / totals[:, :, None])
        .transpose(1, 0, 2)
        .reshape(weighted.shape[1], heads_att * HD)
        .astype(jnp.bfloat16)
        for weighted, totals in results
    ]
    attn_out = rows_out[0]
    return (mamba_out, attn_out)


def solution(mesh):
    in_specs = (
        P("seq", "head"),
        P("seq", "head"),
        P("seq", None),
        P("seq", None),
        P("head", "seq"),
        P("head"),
        P("head"),
        P("head"),
        P("seq", "head"),
        P("seq", "head"),
    )
    out_specs = (P("seq", "head"), P("seq", "head"))
    return jax.shard_map(
        on_device, mesh=mesh, in_specs=in_specs, out_specs=out_specs, check_vma=False
    )
```

profile of v0, /device:TPU:25, one launch (start us, length us, event | category | flops | bytes accessed | tf_op | source)
XLA Modules:
  0.0 200.4 jit_solution(12899004294406485471)
XLA Ops:
  11.2 2.2 %fusion.32 = bf16[16,128,64]{1,2,0:T(8,128)(2,1)} fusion(bf16[256,16,64]{0,2,1:T(8,128)(2,1)S(1)} %bitcast.92, f32[256,16]{0,1:T(8,128)S(1)} %get-tuple-element.482, f32[16]{0:T(128)S(1)} %exponential_multiply_fusion, bf16[256,128]{1,0:T(8,128)(2,1)} %param.18), kind=kOutput, calls=%fused_computation.45 | convolution fusion | flops 403439616 | bytes 868416 | tf_op jit(solution)/shard_map/while/body/eval_jaxpr/hs,sn,shp->hnp/dot_general | solution.py:57
  15.6 13.3 %all-reduce = bf16[128]{0:T(256)(128)(2,1)S(1)} all-reduce(bf16[128]{0:T(256)(128)(2,1)S(1)} %dynamic-update-slice), channel_id=2, replica_groups=mesh['seq'=8,'head'=4] {'seq'}, use_global_device_ids=true, to_apply=%add | all-reduce | flops 128 | bytes 512
  30.1 3.0 %fusion.23 = f32[256,16,64]{0,2,1:T(8,128)S(1)} fusion(bf16[256,16,64]{0,2,1:T(8,128)(2,1)S(1)} %bitcast.93, f32[256,256]{1,0:T(8,128)S(1)} %fusion.47, f32[16,256]{1,0:T(8,128)S(1)} %copy_bitcast_fusion.1, pred[256,256]{1,0:T(8,128)(4,1)S(1)} %iota_compare_fusion), kind=kOutput, calls=%fused_computation.32 | convolution fusion | flops 808452096 | bytes 1916928 | tf_op jit(solution)/shard_map/while/body/eval_jaxpr/hts,shp->thp/dot_general | solution.py:49
  33.7 9.1 %all-gather.10.cloned.1.call-done = bf16[128,128,64]{1,2,0:T(8,128)(2,1)} async-done(((bf16[16,128,64]{1,2,0:T(8,128)(2,1)}), bf16[128,128,64]{1,2,0:T(8,128)(2,1)}) %all-gather.10.cloned.1.call-update) | async-done | bytes 2097168 | tf_op jit(solution)/shard_map/all_gather | solution.py:18
  42.8 13.6 %while.37 = (s32[]{:T(128)}, f32[16,128,64]{2,1,0:T(8,128)S(1)}, s32[]{:T(128)}, bf16[8,16]{1,0:T(8,128)(2,1)S(1)}, bf16[8,16,128,64]{2,3,1,0:T(8,128)(2,1)}, /*index=5*/s32[]{:T(128)}, s32[]{:T(128)}) while((s32[]{:T(128)}, f32[16,128,64]{2,1,0:T(8,128)S(1)}, s32[]{:T(128)}, bf16[8,16]{1,0:T(8,128)(2,1)S(1)}, ...), condition=%wide.region_4.5_spmd.clone, body=%wide.region_3.4_spmd.clone.sunk | while | flops 655380 | bytes 2359569 | solution.py:35
  56.4 2.1 %fusion.28 = f32[256,16,64]{0,2,1:T(8,128)} fusion(f32[256,16,64]{0,2,1:T(8,128)S(1)} %fusion.30, f32[16,128,64]{2,1,0:T(8,128)S(1)} %get-tuple-element.383, bf16[256,16,64]{0,2,1:T(8,128)(2,1)S(1)} %bitcast.94, f32[16]{0:T(128)S(1)} %copy-done.5, f32[256,16]{0,1:T(8,128)S(1)} %get-tuple-element.483, bf16[256,128]{1,0:T(8,128)(2,1)S(1)} %copy-done), kind=kOutput, calls=%fused_computation.36 | convolution fusion | flops 403963904 | bytes 3227712 | tf_op jit(solution)/shard_map/tn,hnp->thp/dot_general | solution.py:133
  58.5 1.6 copy.59
  60.6 7.8 %psum.7 = f32[256]{0:T(256)S(1)} all-reduce(f32[256]{0:T(256)S(1)} %multiply_reduce_fusion), channel_id=1, replica_groups=mesh['seq'=8,'head'=4] {'head'}, use_global_device_ids=true, to_apply=%region_6.7 | all-reduce | flops 256 | bytes 2048 | tf_op jit(solution)/shard_map/psum | solution.py:140
  71.3 44.5 %all-gather.8.cloned.1.call-done = bf16[2048,1024]{1,0:T(8,128)(2,1)} async-done(((bf16[256,1024]{1,0:T(8,128)(2,1)}), bf16[2048,1024]{1,0:T(8,128)(2,1)}) %all-gather.8.cloned.1.call-update) | async-done | bytes 4194320 | tf_op jit(solution)/shard_map/all_gather | solution.py:157
  115.8 6.5 %copy.63 = bf16[2048,1024]{0,1:T(8,128)(2,1)} copy(bf16[2048,1024]{1,0:T(8,128)(2,1)} %all-gather.8.cloned.1.call-done) | data formatting | bytes 8388608 | tf_op jit(solution)/shard_map/while | solution.py:189
  122.3 41.8 %all-gather.6.cloned.1.call-done = bf16[2048,1024]{0,1:T(8,128)(2,1)} async-done(((bf16[256,1024]{0,1:T(8,128)(2,1)}), bf16[2048,1024]{0,1:T(8,128)(2,1)}) %all-gather.6.cloned.1.call-update) | async-done | bytes 4194320 | tf_op jit(solution)/shard_map/all_gather | solution.py:156
  164.2 28.6 %while.36 = (s32[]{:T(128)}, f32[8,256]{1,0:T(8,128)S(1)}, f32[8,256]{1,0:T(8,128)S(1)}, f32[8,256,128]{2,1,0:T(8,128)S(1)}, s32[256]{0:T(256)S(1)}, /*index=5*/...) while((s32[]{:T(128)}, f32[8,256]{1,0:T(8,128)S(1)}, ...), condition=%wide.region_12.13_spmd, body=%wide.region_7.12_spmd.sunk | while | flops 551162368 | bytes 22160680 | solution.py:189
  165.3 6.0 %conditional.2 = (f32[8,256]{1,0:T(8,128)S(1)}, f32[8,256]{1,0:T(8,128)S(1)}, f32[8,256,128]{2,1,0:T(8,128)S(1)}) conditional(s32[]{:T(128)} %convert_element_type.129, (s32[]{:T(128)}, s32[512]{0:T(512)S(1)}, s32[256]{0:T(256)S(1)}, bf16[2048,1024]{0,1:T(8,128)(2,1)}, bf16[256,8,128]{2,0,1:T(8,128)(2,1)S(1)}, /*index=5*/f32[8,256]{1,0:T(8,128)S(1)}, ...), branch_computations={%region_8.10_spmd, %region_11.11_spmd} | conditional | flops 551162368 | bytes 22142018 | solution.py:101
  165.5 1.7 constant_dynamic-slice_fusion
  169.2 2.1 %fusion.6 = f32[8,256,128]{2,1,0:T(8,128)S(1)} fusion(bf16[512,8,128]{0,2,1:T(8,128)(2,1)S(1)} %bitcast.91, f32[8,512,256]{2,1,0:T(8,128)S(1)} %get-tuple-element.477, f32[8,256]{1,0:T(8,128)S(1)} %max.5, pred[256,512]{0,1:T(8,128)(4,1)S(1)} %broadcast_compare_fusion, f32[8,256,128]{2,1,0:T(8,128)S(1)} %get-tuple-element.364, ...), kind=kOutput, calls=%fused_computation.7 | convolution fusion | flops 274202624 | bytes 7487488 | tf_op jit(solution)/shard_map/while/body/eval_jaxpr/cond/branch_0_fun/hqk,khd->hqd/dot_general | solution.py:94
  172.5 6.0 %conditional.2 = (f32[8,256]{1,0:T(8,128)S(1)}, f32[8,256]{1,0:T(8,128)S(1)}, f32[8,256,128]{2,1,0:T(8,128)S(1)}) conditional(s32[]{:T(128)} %convert_element_type.129, (s32[]{:T(128)}, s32[512]{0:T(512)S(1)}, s32[256]{0:T(256)S(1)}, bf16[2048,1024]{0,1:T(8,128)(2,1)}, bf16[256,8,128]{2,0,1:T(8,128)(2,1)S(1)}, /*index=5*/f32[8,256]{1,0:T(8,128)S(1)}, ...), branch_computations={%region_8.10_spmd, %region_11.11_spmd} | conditional | flops 551162368 | bytes 22142018 | solution.py:101
  172.7 1.7 constant_dynamic-slice_fusion
  176.3 2.1 %fusion.6 = f32[8,256,128]{2,1,0:T(8,128)S(1)} fusion(bf16[512,8,128]{0,2,1:T(8,128)(2,1)S(1)} %bitcast.91, f32[8,512,256]{2,1,0:T(8,128)S(1)} %get-tuple-element.477, f32[8,256]{1,0:T(8,128)S(1)} %max.5, pred[256,512]{0,1:T(8,128)(4,1)S(1)} %broadcast_compare_fusion, f32[8,256,128]{2,1,0:T(8,128)S(1)} %get-tuple-element.364, ...), kind=kOutput, calls=%fused_computation.7 | convolution fusion | flops 274202624 | bytes 7487488 | tf_op jit(solution)/shard_map/while/body/eval_jaxpr/cond/branch_0_fun/hqk,khd->hqd/dot_general | solution.py:94
  179.6 6.0 %conditional.2 = (f32[8,256]{1,0:T(8,128)S(1)}, f32[8,256]{1,0:T(8,128)S(1)}, f32[8,256,128]{2,1,0:T(8,128)S(1)}) conditional(s32[]{:T(128)} %convert_element_type.129, (s32[]{:T(128)}, s32[512]{0:T(512)S(1)}, s32[256]{0:T(256)S(1)}, bf16[2048,1024]{0,1:T(8,128)(2,1)}, bf16[256,8,128]{2,0,1:T(8,128)(2,1)S(1)}, /*index=5*/f32[8,256]{1,0:T(8,128)S(1)}, ...), branch_computations={%region_8.10_spmd, %region_11.11_spmd} | conditional | flops 551162368 | bytes 22142018 | solution.py:101
  179.8 1.7 constant_dynamic-slice_fusion
  183.5 2.1 %fusion.6 = f32[8,256,128]{2,1,0:T(8,128)S(1)} fusion(bf16[512,8,128]{0,2,1:T(8,128)(2,1)S(1)} %bitcast.91, f32[8,512,256]{2,1,0:T(8,128)S(1)} %get-tuple-element.477, f32[8,256]{1,0:T(8,128)S(1)} %max.5, pred[256,512]{0,1:T(8,128)(4,1)S(1)} %broadcast_compare_fusion, f32[8,256,128]{2,1,0:T(8,128)S(1)} %get-tuple-element.364, ...), kind=kOutput, calls=%fused_computation.7 | convolution fusion | flops 274202624 | bytes 7487488 | tf_op jit(solution)/shard_map/while/body/eval_jaxpr/cond/branch_0_fun/hqk,khd->hqd/dot_general | solution.py:94
  186.8 6.0 %conditional.2 = (f32[8,256]{1,0:T(8,128)S(1)}, f32[8,256]{1,0:T(8,128)S(1)}, f32[8,256,128]{2,1,0:T(8,128)S(1)}) conditional(s32[]{:T(128)} %convert_element_type.129, (s32[]{:T(128)}, s32[512]{0:T(512)S(1)}, s32[256]{0:T(256)S(1)}, bf16[2048,1024]{0,1:T(8,128)(2,1)}, bf16[256,8,128]{2,0,1:T(8,128)(2,1)S(1)}, /*index=5*/f32[8,256]{1,0:T(8,128)S(1)}, ...), branch_computations={%region_8.10_spmd, %region_11.11_spmd} | conditional | flops 551162368 | bytes 22142018 | solution.py:101
  187.0 1.7 constant_dynamic-slice_fusion
  190.6 2.1 %fusion.6 = f32[8,256,128]{2,1,0:T(8,128)S(1)} fusion(bf16[512,8,128]{0,2,1:T(8,128)(2,1)S(1)} %bitcast.91, f32[8,512,256]{2,1,0:T(8,128)S(1)} %get-tuple-element.477, f32[8,256]{1,0:T(8,128)S(1)} %max.5, pred[256,512]{0,1:T(8,128)(4,1)S(1)} %broadcast_compare_fusion, f32[8,256,128]{2,1,0:T(8,128)S(1)} %get-tuple-element.364, ...), kind=kOutput, calls=%fused_computation.7 | convolution fusion | flops 274202624 | bytes 7487488 | tf_op jit(solution)/shard_map/while/body/eval_jaxpr/cond/branch_0_fun/hqk,khd->hqd/dot_general | solution.py:94
  (117 shorter events, 35.6 us)
Async XLA Ops:
  7.2 21.9 %copy-start = (bf16[256,128]{1,0:T(8,128)(2,1)S(1)}, bf16[256,128]{1,0:T(8,128)(2,1)}, u32[]{:S(2)}) copy-start(bf16[256,128]{1,0:T(8,128)(2,1)} %param.19) | copy-start | bytes 196612
  7.2 35.6 %all-gather.10.cloned.1.call-start = ((), (), s32[]{:S(2)}) async-start(), calls=%async_computation.2 | async-start | bytes 2359296 | tf_op jit(solution)/shard_map/all_gather | solution.py:18
  13.4 102.4 %all-gather.8.cloned.1.call-start = ((), (), s32[]{:S(2)}) async-start(), calls=%async_computation.1 | async-start | bytes 4718592 | tf_op jit(solution)/shard_map/all_gather | solution.py:157
  42.8 13.6 %copy-start.5 = (f32[16]{0:T(128)S(1)}, f32[16]{0:T(128)}, u32[]{:S(2)}) copy-start(f32[16]{0:T(128)} %param.22) | copy-start | bytes 196
  56.4 3.8 %copy-start.1 = (bf16[256,1024]{1,0:T(8,128)(2,1)S(1)}, bf16[256,1024]{1,0:T(8,128)(2,1)}, u32[]{:S(2)}) copy-start(bf16[256,1024]{1,0:T(8,128)(2,1)} %param.17) | copy-start | bytes 1572868
  56.4 12.0 %copy-start.4 = (f32[1024]{0:T(1024)S(1)}, f32[1024]{0:T(1024)}, u32[]{:S(2)}) copy-start(f32[1024]{0:T(1024)} %param.23) | copy-start | bytes 12292
  58.5 11.3 %copy-start.2 = (bf16[256,1024]{1,0:T(8,128)(2,1)S(1)}, bf16[256,1024]{1,0:T(8,128)(2,1)}, u32[]{:S(2)}) copy-start(bf16[256,1024]{1,0:T(8,128)(2,1)} %param.25) | copy-start | bytes 1572868
  58.5 12.3 %copy-start.3 = (bf16[256,1024]{1,0:T(8,128)(2,1)S(1)}, bf16[256,1024]{1,0:T(8,128)(2,1)}, u32[]{:S(2)}) copy-start(bf16[256,1024]{1,0:T(8,128)(2,1)} %param.24) | copy-start | bytes 1572868
  69.5 94.6 %all-gather.6.cloned.1.call-start = ((), (), s32[]{:S(2)}) async-start(), calls=%async_computation | async-start | bytes 4718592 | tf_op jit(solution)/shard_map/all_gather | solution.py:156
Sparse Core Ops, SparseCore 0:
  13.5 29.2 all-gather.9
  69.7 46.0 all-gather.7
  118.0 46.0 all-gather.5
where the time goes:
time: 201 us; the launch traced here: 200 us
  waiting for transfers between devices  95.4 us (47%)
  local copies, waits for them, and re-layouts  32 us (16%)
  blocking collectives  21.1 us (10%)
  matrix products  21 us (10%)
  between operations  14.6 us (7%)
  other arithmetic  12.9 us (6%)
  loops' own time  3.13 us (2%)
    all_gather x1, waiting for transfers between devices, on_device(): v_piece = lax.all_gather(mamba_out, 'seq', axis=0, tiled=True)  44.5 us
    all_gather x1, waiting for transfers between devices, on_device(): k_piece = lax.all_gather(keys, 'seq', axis=0, tiled=True)  41.8 us
    unnamed x1, blocking collectives  13.3 us
    dynamic_slice x16, local copies, waits for them, and re-layouts, hop(): part[k].astype(own.dtype)  10.1 us
    all_gather x1, waiting for transfers between devices, carried_in(): lax.all_gather(part.astype(kind), axis)  9.1 us
    dot_general x4, matrix products, online_update(): jnp.einsum('hqk,khd->hqd', weights.astype(jnp.bfloat16), v_rows, preferre...  8.4 us
    psum x1, blocking collectives, on_device(): squares = lax.psum(jnp.sum(gated * gated, axis=1), 'head')  7.76 us
    while x2, local copies, waits for them, and re-layouts, on_device(): finals = lax.fori_loop(0, row_count // block_rows, one_block, states)  6.79 us
  transfers between devices with their start and end apart: 3, of which 3 were waited for; matrix products, arithmetic and copies ran while one was open for 7% of the time, Pallas kernels for 0%

commit v1 on v0

--- a/solution.py
+++ b/solution.py
@@ -153,7 +153,19 @@
         )
     )
     states = initial
-    k_piece = lax.all_gather(keys, "seq", axis=0, tiled=True)
+    ways, here, lap = (lax.axis_size("seq"), lax.axis_index("seq"), keys.shape[0])
+    dims = [n * ways if d == 0 else n for d, n in enumerate(keys.shape)]
+    full = lax.dynamic_update_slice_in_dim(jnp.zeros(dims, keys.dtype), keys, here * lap, axis=0)
+    going_up = going_down = keys
+    for far in range(1, ways // 2 + 1):
+        going_up = lax.ppermute(going_up, "seq", [(d, (d + 1) % ways) for d in range(ways)])
+        full = lax.dynamic_update_slice_in_dim(full, going_up, (here - far) % ways * lap, axis=0)
+        if 2 * far < ways:
+            going_down = lax.ppermute(going_down, "seq", [(d, (d - 1) % ways) for d in range(ways)])
+            full = lax.dynamic_update_slice_in_dim(
+                full, going_down, (here + far) % ways * lap, axis=0
+            )
+    k_piece = full
     v_piece = lax.all_gather(mamba_out, "seq", axis=0, tiled=True)
     row_count = k_piece.shape[0]
     block_rows = math.gcd(row_count, 512)

time: 201 us -> 194 us (0.965)
  waiting for transfers between devices: 95.4 us -> 52.9 us
  starting transfers between devices: 0.3 us -> 23.1 us
  local copies, waits for them, and re-layouts: 32 us -> 42.9 us
    all_gather x1, waiting for transfers between devices: 44.5 us -> 0.01 us  [on_device(): v_piece = lax.all_gather(mamba_out, 'seq', axis=0, tiled=True)]
    ppermute x0 -> x7, waiting for transfers between devices: none -> 43.8 us  [the longest x4 40 us: on_device(): lax.ppermute(going_up, 'seq', [(d, (d + 1) % ways) for d in range(ways)])]
    all_gather x1 -> x0, waiting for transfers between devices: 41.8 us -> none  [on_device(): k_piece = lax.all_gather(keys, 'seq', axis=0, tiled=True)]
    ppermute x0 -> x7, starting transfers between devices: none -> 23 us  [the longest x4 16.7 us: on_device(): lax.ppermute(going_up, 'seq', [(d, (d + 1) % ways) for d in range(ways)])]
    dynamic_update_slice x0 -> x8, local copies, waits for them, and re-layouts: none -> 9.07 us  [the longest x4 4.56 us: on_device(): lax.dynamic_update_slice_in_dim(full, going_up, (here - far) % ways * lap...]
    broadcast_in_dim x0 -> x1, local copies, waits for them, and re-layouts: none -> 2.48 us  [on_device(): jnp.zeros(dims, keys.dtype)]
  transfers between devices with their start and end apart: 3 -> 9, of which waited for: 3 -> 5; matrix products, arithmetic and copies ran while one was open for 7% -> 10% of each run, Pallas kernels for 0% -> 0%
where the time goes in v1:
time: 194 us; the launch traced here: 192 us
  waiting for transfers between devices  52.9 us (27%)
  local copies, waits for them, and re-layouts  42.9 us (22%)
  starting transfers between devices  23.1 us (12%)
  blocking collectives  21.1 us (11%)
  matrix products  21 us (11%)
  between operations  14.9 us (8%)
  other arithmetic  12.9 us (7%)
  loops' own time  3.41 us (2%)
    ppermute x4, waiting for transfers between devices, on_device(): lax.ppermute(going_up, 'seq', [(d, (d + 1) % ways) for d in range(ways)])  40 us
    ppermute x4, starting transfers between devices, on_device(): lax.ppermute(going_up, 'seq', [(d, (d + 1) % ways) for d in range(ways)])  16.7 us
    unnamed x1, blocking collectives  13.3 us
    dynamic_slice x16, local copies, waits for them, and re-layouts, hop(): part[k].astype(own.dtype)  10.1 us
    all_gather x1, waiting for transfers between devices, carried_in(): lax.all_gather(part.astype(kind), axis)  9.12 us
    dot_general x4, matrix products, online_update(): jnp.einsum('hqk,khd->hqd', weights.astype(jnp.bfloat16), v_rows, preferre...  8.43 us
    psum x1, blocking collectives, on_device(): squares = lax.psum(jnp.sum(gated * gated, axis=1), 'head')  7.77 us
    while x2, local copies, waits for them, and re-layouts, on_device(): finals = lax.fori_loop(0, row_count // block_rows, one_block, states)  6.78 us
  transfers between devices with their start and end apart: 9, of which 5 were waited for; matrix products, arithmetic and copies ran while one was open for 10% of the time, Pallas kernels for 0%

profile of v1, /device:TPU:25, one launch (start us, length us, event | category | flops | bytes accessed | tf_op | source)
XLA Modules:
  0.0 192.3 jit_solution(11299126646701555441)
XLA Ops:
  11.2 2.2 %fusion.32 = bf16[16,128,64]{1,2,0:T(8,128)(2,1)} fusion(bf16[256,16,64]{0,2,1:T(8,128)(2,1)S(1)} %bitcast.92, f32[256,16]{0,1:T(8,128)S(1)} %get-tuple-element.482, f32[16]{0:T(128)S(1)} %exponential_multiply_fusion, bf16[256,128]{1,0:T(8,128)(2,1)} %param.18), kind=kOutput, calls=%fused_computation.45 | convolution fusion | flops 403439616 | bytes 868416 | tf_op jit(solution)/shard_map/while/body/eval_jaxpr/hs,sn,shp->hnp/dot_general | solution.py:57
  15.6 13.3 %all-reduce = bf16[128]{0:T(256)(128)(2,1)S(1)} all-reduce(bf16[128]{0:T(256)(128)(2,1)S(1)} %dynamic-update-slice), channel_id=2, replica_groups=mesh['seq'=8,'head'=4] {'seq'}, use_global_device_ids=true, to_apply=%add | all-reduce | flops 128 | bytes 512
  30.1 3.0 %fusion.23 = f32[256,16,64]{0,2,1:T(8,128)S(1)} fusion(bf16[256,16,64]{0,2,1:T(8,128)(2,1)S(1)} %bitcast.93, f32[256,256]{1,0:T(8,128)S(1)} %fusion.47, f32[16,256]{1,0:T(8,128)S(1)} %copy_bitcast_fusion.1, pred[256,256]{1,0:T(8,128)(4,1)S(1)} %iota_compare_fusion), kind=kOutput, calls=%fused_computation.32 | convolution fusion | flops 808452096 | bytes 1916928 | tf_op jit(solution)/shard_map/while/body/eval_jaxpr/hts,shp->thp/dot_general | solution.py:49
  33.7 9.1 %all-gather.7.cloned.1.call-done = bf16[128,128,64]{1,2,0:T(8,128)(2,1)} async-done(((bf16[16,128,64]{1,2,0:T(8,128)(2,1)}), bf16[128,128,64]{1,2,0:T(8,128)(2,1)}) %all-gather.7.cloned.1.call-update) | async-done | bytes 2097168 | tf_op jit(solution)/shard_map/all_gather | solution.py:18
  42.8 13.6 %while.37 = (s32[]{:T(128)}, f32[16,128,64]{2,1,0:T(8,128)S(1)}, s32[]{:T(128)}, bf16[8,16]{1,0:T(8,128)(2,1)S(1)}, bf16[8,16,128,64]{2,3,1,0:T(8,128)(2,1)}, /*index=5*/s32[]{:T(128)}, s32[]{:T(128)}) while((s32[]{:T(128)}, f32[16,128,64]{2,1,0:T(8,128)S(1)}, s32[]{:T(128)}, bf16[8,16]{1,0:T(8,128)(2,1)S(1)}, ...), condition=%wide.region_4.5_spmd.clone, body=%wide.region_3.4_spmd.clone.sunk | while | flops 655380 | bytes 2359569 | solution.py:35
  60.6 7.8 %psum.7 = f32[256]{0:T(256)S(1)} all-reduce(f32[256]{0:T(256)S(1)} %multiply_reduce_fusion), channel_id=1, replica_groups=mesh['seq'=8,'head'=4] {'head'}, use_global_device_ids=true, to_apply=%region_6.7 | all-reduce | flops 256 | bytes 2048 | tf_op jit(solution)/shard_map/psum | solution.py:140
  69.8 3.8 %collective-permute-start = (bf16[256,1024]{0,1:T(8,128)(2,1)S(1)}, bf16[256,1024]{0,1:T(8,128)(2,1)S(1)}, u32[]{:S(2)}, u32[]{:S(2)}) collective-permute-start(bf16[256,1024]{0,1:T(8,128)(2,1)S(1)} %copy.64), channel_id=1, source_target_pairs={{0,4},{4,8},{8,12},{12,16},{16,20},{20,24},{24,28},{28,0},{1,5},{5... | collective-permute-start | bytes 1572872 | tf_op jit(solution)/shard_map/ppermute | solution.py:161
  73.6 17.1 %collective-permute-done = bf16[256,1024]{0,1:T(8,128)(2,1)S(1)} collective-permute-done((bf16[256,1024]{0,1:T(8,128)(2,1)S(1)}, bf16[256,1024]{0,1:T(8,128)(2,1)S(1)}, u32[]{:S(2)}, u32[]{:S(2)}) %collective-permute-start) | collective-permute-done | bytes 524320 | tf_op jit(solution)/shard_map/ppermute | solution.py:161
  90.7 4.3 %collective-permute-start.2 = (bf16[256,1024]{0,1:T(8,128)(2,1)S(1)}, bf16[256,1024]{0,1:T(8,128)(2,1)}, u32[]{:S(2)}, u32[]{:S(2)}) collective-permute-start(bf16[256,1024]{0,1:T(8,128)(2,1)S(1)} %collective-permute-done), channel_id=1, source_target_pairs={{0,4},{4,8},{8,12},{12,16},{16,20},{20,24},{24,28},{28,0},{1,5},{5... | collective-permute-start | bytes 1572872 | tf_op jit(solution)/shard_map/ppermute | solution.py:161
  94.9 3.8 %collective-permute-done.1 = bf16[256,1024]{0,1:T(8,128)(2,1)S(1)} collective-permute-done((bf16[256,1024]{0,1:T(8,128)(2,1)S(1)}, bf16[256,1024]{0,1:T(8,128)(2,1)S(1)}, u32[]{:S(2)}, u32[]{:S(2)}) %collective-permute-start.1) | collective-permute-done | bytes 524320 | tf_op jit(solution)/shard_map/ppermute | solution.py:164
  98.8 18.9 %collective-permute-done.2 = bf16[256,1024]{0,1:T(8,128)(2,1)} collective-permute-done((bf16[256,1024]{0,1:T(8,128)(2,1)S(1)}, bf16[256,1024]{0,1:T(8,128)(2,1)}, u32[]{:S(2)}, u32[]{:S(2)}) %collective-permute-start.2) | collective-permute-done | bytes 524320 | tf_op jit(solution)/shard_map/ppermute | solution.py:161
  117.6 4.4 %collective-permute-start.4 = (bf16[256,1024]{0,1:T(8,128)(2,1)}, bf16[256,1024]{0,1:T(8,128)(2,1)S(1)}, u32[]{:S(2)}, u32[]{:S(2)}) collective-permute-start(bf16[256,1024]{0,1:T(8,128)(2,1)} %collective-permute-done.2), channel_id=1, source_target_pairs={{0,4},{4,8},{8,12},{12,16},{16,20},{20,24},{24,28},{28,0},{1,5},{5... | collective-permute-start | bytes 1572872 | tf_op jit(solution)/shard_map/ppermute | solution.py:161
  122.6 2.5 %broadcast_in_dim.94 = bf16[2048,1024]{0,1:T(8,128)(2,1)} broadcast(bf16[]{:T(256)} %constant.170.clone.1), dimensions={} | broadcast | bytes 4194306 | tf_op jit(solution)/shard_map/broadcast_in_dim | solution.py:158
  125.9 6.3 %collective-permute-start.5 = (bf16[256,1024]{0,1:T(8,128)(2,1)}, bf16[256,1024]{0,1:T(8,128)(2,1)S(1)}, u32[]{:S(2)}, u32[]{:S(2)}) collective-permute-start(bf16[256,1024]{0,1:T(8,128)(2,1)} %collective-permute-done.3), channel_id=1, source_target_pairs={{0,28},{4,0},{8,4},{12,8},{16,12},{20,16},{24,20},{28,24},{1,29},{... | collective-permute-start | bytes 1572872 | tf_op jit(solution)/shard_map/ppermute | solution.py:164
  133.1 4.0 %collective-permute-done.4 = bf16[256,1024]{0,1:T(8,128)(2,1)S(1)} collective-permute-done((bf16[256,1024]{0,1:T(8,128)(2,1)}, bf16[256,1024]{0,1:T(8,128)(2,1)S(1)}, u32[]{:S(2)}, u32[]{:S(2)}) %collective-permute-start.4) | collective-permute-done | bytes 524320 | tf_op jit(solution)/shard_map/ppermute | solution.py:161
  137.2 4.2 %collective-permute-start.6 = (bf16[256,1024]{0,1:T(8,128)(2,1)S(1)}, bf16[256,1024]{0,1:T(8,128)(2,1)S(1)}, u32[]{:S(2)}, u32[]{:S(2)}) collective-permute-start(bf16[256,1024]{0,1:T(8,128)(2,1)S(1)} %collective-permute-done.4), channel_id=1, source_target_pairs={{0,4},{4,8},{8,12},{12,16},{16,20},{20,24},{24,28},{28,0},{1,5},{5... | collective-permute-start | bytes 1572872 | tf_op jit(solution)/shard_map/ppermute | solution.py:161
  148.7 6.5 %copy.69 = bf16[2048,1024]{0,1:T(8,128)(2,1)} copy(bf16[2048,1024]{1,0:T(8,128)(2,1)} %all-gather.5.cloned.1.call-done) | data formatting | bytes 8388608 | tf_op jit(solution)/shard_map/while | solution.py:201
  155.3 29.1 %while.36 = (s32[]{:T(128)}, f32[8,256]{1,0:T(8,128)S(1)}, f32[8,256]{1,0:T(8,128)S(1)}, f32[8,256,128]{2,1,0:T(8,128)S(1)}, s32[256]{0:T(256)S(1)}, /*index=5*/...) while((s32[]{:T(128)}, f32[8,256]{1,0:T(8,128)S(1)}, ...), condition=%wide.region_12.13_spmd, body=%wide.region_7.12_spmd.sunk | while | flops 551162368 | bytes 22160688 | solution.py:201
  156.5 6.0 %conditional.2 = (f32[8,256]{1,0:T(8,128)S(1)}, f32[8,256]{1,0:T(8,128)S(1)}, f32[8,256,128]{2,1,0:T(8,128)S(1)}) conditional(s32[]{:T(128)} %convert_element_type.129, (s32[]{:T(128)}, s32[512]{0:T(512)S(1)}, s32[256]{0:T(256)S(1)}, bf16[2048,1024]{0,1:T(8,128)(2,1)}, bf16[256,8,128]{2,0,1:T(8,128)(2,1)S(1)}, /*index=5*/f32[8,256]{1,0:T(8,128)S(1)}, ...), branch_computations={%region_8.10_spmd, %region_11.11_spmd} | conditional | flops 551162368 | bytes 22142018 | solution.py:101
  160.4 2.1 %fusion.6 = f32[8,256,128]{2,1,0:T(8,128)S(1)} fusion(bf16[512,8,128]{0,2,1:T(8,128)(2,1)S(1)} %bitcast.91, f32[8,512,256]{2,1,0:T(8,128)S(1)} %get-tuple-element.477, f32[8,256]{1,0:T(8,128)S(1)} %max.5, pred[256,512]{0,1:T(8,128)(4,1)S(1)} %broadcast_compare_fusion, f32[8,256,128]{2,1,0:T(8,128)S(1)} %get-tuple-element.364, ...), kind=kOutput, calls=%fused_computation.7 | convolution fusion | flops 274202624 | bytes 7487488 | tf_op jit(solution)/shard_map/while/body/eval_jaxpr/cond/branch_0_fun/hqk,khd->hqd/dot_general | solution.py:94
  163.8 6.0 %conditional.2 = (f32[8,256]{1,0:T(8,128)S(1)}, f32[8,256]{1,0:T(8,128)S(1)}, f32[8,256,128]{2,1,0:T(8,128)S(1)}) conditional(s32[]{:T(128)} %convert_element_type.129, (s32[]{:T(128)}, s32[512]{0:T(512)S(1)}, s32[256]{0:T(256)S(1)}, bf16[2048,1024]{0,1:T(8,128)(2,1)}, bf16[256,8,128]{2,0,1:T(8,128)(2,1)S(1)}, /*index=5*/f32[8,256]{1,0:T(8,128)S(1)}, ...), branch_computations={%region_8.10_spmd, %region_11.11_spmd} | conditional | flops 551162368 | bytes 22142018 | solution.py:101
  167.7 2.1 %fusion.6 = f32[8,256,128]{2,1,0:T(8,128)S(1)} fusion(bf16[512,8,128]{0,2,1:T(8,128)(2,1)S(1)} %bitcast.91, f32[8,512,256]{2,1,0:T(8,128)S(1)} %get-tuple-element.477, f32[8,256]{1,0:T(8,128)S(1)} %max.5, pred[256,512]{0,1:T(8,128)(4,1)S(1)} %broadcast_compare_fusion, f32[8,256,128]{2,1,0:T(8,128)S(1)} %get-tuple-element.364, ...), kind=kOutput, calls=%fused_computation.7 | convolution fusion | flops 274202624 | bytes 7487488 | tf_op jit(solution)/shard_map/while/body/eval_jaxpr/cond/branch_0_fun/hqk,khd->hqd/dot_general | solution.py:94
  171.1 6.0 %conditional.2 = (f32[8,256]{1,0:T(8,128)S(1)}, f32[8,256]{1,0:T(8,128)S(1)}, f32[8,256,128]{2,1,0:T(8,128)S(1)}) conditional(s32[]{:T(128)} %convert_element_type.129, (s32[]{:T(128)}, s32[512]{0:T(512)S(1)}, s32[256]{0:T(256)S(1)}, bf16[2048,1024]{0,1:T(8,128)(2,1)}, bf16[256,8,128]{2,0,1:T(8,128)(2,1)S(1)}, /*index=5*/f32[8,256]{1,0:T(8,128)S(1)}, ...), branch_computations={%region_8.10_spmd, %region_11.11_spmd} | conditional | flops 551162368 | bytes 22142018 | solution.py:101
  178.4 6.0 %conditional.2 = (f32[8,256]{1,0:T(8,128)S(1)}, f32[8,256]{1,0:T(8,128)S(1)}, f32[8,256,128]{2,1,0:T(8,128)S(1)}) conditional(s32[]{:T(128)} %convert_element_type.129, (s32[]{:T(128)}, s32[512]{0:T(512)S(1)}, s32[256]{0:T(256)S(1)}, bf16[2048,1024]{0,1:T(8,128)(2,1)}, bf16[256,8,128]{2,0,1:T(8,128)(2,1)S(1)}, /*index=5*/f32[8,256]{1,0:T(8,128)S(1)}, ...), branch_computations={%region_8.10_spmd, %region_11.11_spmd} | conditional | flops 551162368 | bytes 22142018 | solution.py:101
  (141 shorter events, 58.6 us)
Async XLA Ops:
  7.2 21.9 %copy-start = (bf16[256,128]{1,0:T(8,128)(2,1)S(1)}, bf16[256,128]{1,0:T(8,128)(2,1)}, u32[]{:S(2)}) copy-start(bf16[256,128]{1,0:T(8,128)(2,1)} %param.19) | copy-start | bytes 196612
  7.2 35.6 %all-gather.7.cloned.1.call-start = ((), (), s32[]{:S(2)}) async-start(), calls=%async_computation.1 | async-start | bytes 2359296 | tf_op jit(solution)/shard_map/all_gather | solution.py:18
  13.4 135.3 %all-gather.5.cloned.1.call-start = ((), (), s32[]{:S(2)}) async-start(), calls=%async_computation | async-start | bytes 4718592 | tf_op jit(solution)/shard_map/all_gather | solution.py:169
  42.8 13.6 %copy-start.7 = (f32[16]{0:T(128)S(1)}, f32[16]{0:T(128)}, u32[]{:S(2)}) copy-start(f32[16]{0:T(128)} %param.22) | copy-start | bytes 196
  56.4 3.8 %copy-start.1 = (bf16[256,1024]{1,0:T(8,128)(2,1)S(1)}, bf16[256,1024]{1,0:T(8,128)(2,1)}, u32[]{:S(2)}) copy-start(bf16[256,1024]{1,0:T(8,128)(2,1)} %param.17) | copy-start | bytes 1572868
  56.4 11.9 %copy-start.6 = (f32[1024]{0:T(1024)S(1)}, f32[1024]{0:T(1024)}, u32[]{:S(2)}) copy-start(f32[1024]{0:T(1024)} %param.23) | copy-start | bytes 12292
  58.5 11.0 %copy-start.2 = (bf16[256,1024]{1,0:T(8,128)(2,1)S(1)}, bf16[256,1024]{1,0:T(8,128)(2,1)}, u32[]{:S(2)}) copy-start(bf16[256,1024]{1,0:T(8,128)(2,1)} %param.25) | copy-start | bytes 1572868
  58.5 63.5 %copy-start.3 = (bf16[256,1024]{1,0:T(8,128)(2,1)S(1)}, bf16[256,1024]{1,0:T(8,128)(2,1)}, u32[]{:S(2)}) copy-start(bf16[256,1024]{1,0:T(8,128)(2,1)} %param.24) | copy-start | bytes 1572868
  69.8 20.9 %collective-permute-start = (bf16[256,1024]{0,1:T(8,128)(2,1)S(1)}, bf16[256,1024]{0,1:T(8,128)(2,1)S(1)}, u32[]{:S(2)}, u32[]{:S(2)}) collective-permute-start(bf16[256,1024]{0,1:T(8,128)(2,1)S(1)} %copy.64), channel_id=1, source_target_pairs={{0,4},{4,8},{8,12},{12,16},{16,20},{20,24},{24,28},{28,0},{1,5},{5... | collective-permute-start | bytes 1572872 | tf_op jit(solution)/shard_map/ppermute | solution.py:161
  73.6 25.2 %collective-permute-start.1 = (bf16[256,1024]{0,1:T(8,128)(2,1)S(1)}, bf16[256,1024]{0,1:T(8,128)(2,1)S(1)}, u32[]{:S(2)}, u32[]{:S(2)}) collective-permute-start(bf16[256,1024]{0,1:T(8,128)(2,1)S(1)} %copy.64), channel_id=1, source_target_pairs={{0,28},{4,0},{8,4},{12,8},{16,12},{20,16},{24,20},{28,24},{1,29},{... | collective-permute-start | bytes 1572872 | tf_op jit(solution)/shard_map/ppermute | solution.py:164
  90.7 31.6 %copy-start.4 = (bf16[256,1024]{0,1:T(8,128)(2,1)}, bf16[256,1024]{0,1:T(8,128)(2,1)S(1)}, u32[]{:S(2)}) copy-start(bf16[256,1024]{0,1:T(8,128)(2,1)S(1)} %collective-permute-done) | copy-start | bytes 1572868
  90.7 27.0 %collective-permute-start.2 = (bf16[256,1024]{0,1:T(8,128)(2,1)S(1)}, bf16[256,1024]{0,1:T(8,128)(2,1)}, u32[]{:S(2)}, u32[]{:S(2)}) collective-permute-start(bf16[256,1024]{0,1:T(8,128)(2,1)S(1)} %collective-permute-done), channel_id=1, source_target_pairs={{0,4},{4,8},{8,12},{12,16},{16,20},{20,24},{24,28},{28,0},{1,5},{5... | collective-permute-start | bytes 1572872 | tf_op jit(solution)/shard_map/ppermute | solution.py:161
  98.8 27.2 %collective-permute-start.3 = (bf16[256,1024]{0,1:T(8,128)(2,1)S(1)}, bf16[256,1024]{0,1:T(8,128)(2,1)}, u32[]{:S(2)}, u32[]{:S(2)}) collective-permute-start(bf16[256,1024]{0,1:T(8,128)(2,1)S(1)} %collective-permute-done.1), channel_id=1, source_target_pairs={{0,28},{4,0},{8,4},{12,8},{16,12},{20,16},{24,20},{28,24},{1,29},{... | collective-permute-start | bytes 1572872 | tf_op jit(solution)/shard_map/ppermute | solution.py:164
  117.6 19.5 %collective-permute-start.4 = (bf16[256,1024]{0,1:T(8,128)(2,1)}, bf16[256,1024]{0,1:T(8,128)(2,1)S(1)}, u32[]{:S(2)}, u32[]{:S(2)}) collective-permute-start(bf16[256,1024]{0,1:T(8,128)(2,1)} %collective-permute-done.2), channel_id=1, source_target_pairs={{0,4},{4,8},{8,12},{12,16},{16,20},{20,24},{24,28},{28,0},{1,5},{5... | collective-permute-start | bytes 1572872 | tf_op jit(solution)/shard_map/ppermute | solution.py:161
  122.3 10.0 %copy-start.5 = (bf16[256,1024]{0,1:T(8,128)(2,1)S(1)}, bf16[256,1024]{0,1:T(8,128)(2,1)}, u32[]{:S(2)}) copy-start(bf16[256,1024]{0,1:T(8,128)(2,1)} %copy-done.4) | copy-start | bytes 1572868
  125.9 21.0 %collective-permute-start.5 = (bf16[256,1024]{0,1:T(8,128)(2,1)}, bf16[256,1024]{0,1:T(8,128)(2,1)S(1)}, u32[]{:S(2)}, u32[]{:S(2)}) collective-permute-start(bf16[256,1024]{0,1:T(8,128)(2,1)} %collective-permute-done.3), channel_id=1, source_target_pairs={{0,28},{4,0},{8,4},{12,8},{16,12},{20,16},{24,20},{28,24},{1,29},{... | collective-permute-start | bytes 1572872 | tf_op jit(solution)/shard_map/ppermute | solution.py:164
  137.2 10.7 %collective-permute-start.6 = (bf16[256,1024]{0,1:T(8,128)(2,1)S(1)}, bf16[256,1024]{0,1:T(8,128)(2,1)S(1)}, u32[]{:S(2)}, u32[]{:S(2)}) collective-permute-start(bf16[256,1024]{0,1:T(8,128)(2,1)S(1)} %collective-permute-done.4), channel_id=1, source_target_pairs={{0,4},{4,8},{8,12},{12,16},{16,20},{20,24},{24,28},{28,0},{1,5},{5... | collective-permute-start | bytes 1572872 | tf_op jit(solution)/shard_map/ppermute | solution.py:161
Sparse Core Ops, SparseCore 0:
  13.6 29.2 all-gather.6
  69.7 64.5 all-gather.4
